TPU v7x, 32 devices: a whole 2x2x4 slice. The times are simulated.
32 devices in a mesh: gx: 8 (over y, x, core), gy: 4 (over z).
Axes of the slice: x: 2, y: 2, z: 4, core: 2. Of those that a mesh axis runs over, the one named last changes fastest.
Arguments:
- particle_count: int32 [8, 256, 1024], P(None, ('gx', 'gy')), may hold values from 0 to 12
- drag_coeff: float32 [8, 256, 1024], P(None, ('gx', 'gy')), may hold values from 0.05 to 2
- particle_velocity: float32 [3, 8, 256, 1024], P(None, None, ('gx', 'gy')), may hold values from -6 to 6
- fluid_velocity: float32 [3, 8, 256, 1024], P(None, None, 'gy', 'gx'), may hold values from -6 to 6
Outputs:
- pressure: float32 [8, 256, 1024], P(None, 'gy', 'gx')
- new_velocity: float32 [3, 8, 256, 1024], P(None, None, ('gx', 'gy'))
- pressure_gradient: float32 [3, 8, 256, 1024], P(None, None, ('gx', 'gy'))
All inputs are finite; a program needn't handle non-finite values.
Results may differ from a plain program's by a relative error of at most 0.00002.
Values sent between devices are 32-bit elements; how exact they have to be, the bound alone decides.
A program may use at most 64 MiB of HBM per device.

v0:
```python
import jax
import jax.numpy as jnp
from jax import lax
from jax.sharding import PartitionSpec as P

SWEEPS = 8
particle_volume = 0.05
time_step = 0.5
viscosity = 0.1


def padded_2(cells, sides, width):
    for axis, dim in sides:
        count = lax.axis_size(axis)
        ends = count - 1
        head = lax.slice_in_dim(cells, 0, width, axis=dim)
        tail = lax.slice_in_dim(cells, cells.shape[dim] - width, cells.shape[dim], axis=dim)
        cells = jnp.concatenate(
            [
                lax.ppermute(tail, axis, [(i, (i + 1) % count) for i in range(ends)]),
                cells,
                lax.ppermute(head, axis, [((i + 1) % count, i) for i in range(ends)]),
            ],
            axis=dim,
        )
    return cells


def pad_depth(values):
    widths = [(0, 0)] * (values.ndim - 3) + [(1, 1), (0, 0), (0, 0)]
    return jnp.pad(values, widths)


def pad_plane(values):
    widths = [(0, 0)] * (values.ndim - 2) + [(1, 1), (1, 1)]
    return jnp.pad(values, widths)


def pad_second(values):
    widths = [(0, 0)] * (values.ndim - 1) + [(1, 1)]
    return jnp.pad(values, widths)


def middle(values):
    return values[..., 1:-1, 1:-1, 1:-1]


def neighbour(values, which):
    if which == 0:
        return values[..., 2:, 1:-1, 1:-1]
    if which == 1:
        return values[..., :-2, 1:-1, 1:-1]
    if which == 2:
        return values[..., 1:-1, 2:, 1:-1]
    if which == 3:
        return values[..., 1:-1, :-2, 1:-1]
    if which == 4:
        return values[..., 1:-1, 1:-1, 2:]
    return values[..., 1:-1, 1:-1, :-2]


def face_weights(voids_wide):
    padded = pad_depth(voids_wide)
    centre = middle(padded)
    weights = jnp.stack([0.5 * (centre + neighbour(padded, which)) for which in range(6)])
    weight_sum = weights[0]
    for which in range(1, 6):
        weight_sum = weight_sum + weights[which]
    return (weights, weight_sum)


def momentum(velocity_wide, weights, voids, drag, drag_force):
    padded = pad_depth(velocity_wide)
    centre = middle(padded)
    diffusion = jnp.zeros_like(centre)
    for which in range(6):
        diffusion = diffusion + weights[which][None] * (neighbour(padded, which) - centre)
    return (voids[None] * centre + time_step * viscosity * diffusion + time_step * drag_force) / (
        voids[None] + time_step * drag[None]
    )


def divergence(flux_wide):
    first = flux_wide[0][:, 2:, 1:-1] - flux_wide[0][:, :-2, 1:-1]
    second = flux_wide[1][:, 1:-1, 2:] - flux_wide[1][:, 1:-1, :-2]
    normal = pad_depth(flux_wide[2])[:, 1:-1, 1:-1]
    third = normal[2:] - normal[:-2]
    return 0.5 * (first + second + third) / time_step


def jacobi_sweep(pressure_wide, weights, weight_sum, source):
    padded = pad_depth(pressure_wide)
    total = weights[0] * neighbour(padded, 0)
    for which in range(1, 6):
        total = total + weights[which] * neighbour(padded, which)
    return (total - source) / weight_sum


def gradient_of(pressure_wide):
    padded = pad_depth(pressure_wide)
    first = 0.5 * (padded[1:-1, 2:, 1:-1] - padded[1:-1, :-2, 1:-1])
    second = 0.5 * (padded[1:-1, 1:-1, 2:] - padded[1:-1, 1:-1, :-2])
    third = 0.5 * (padded[2:, 1:-1, 1:-1] - padded[:-2, 1:-1, 1:-1])
    return jnp.stack([first, second, third])


def order_inward(values, across, along):
    fields, planes, x_rows, y_cols = values.shape
    groups = across // along
    rows_each = x_rows // across
    shaped = values.reshape(fields, planes, along, groups, rows_each, y_cols)
    return jnp.swapaxes(shaped, 2, 3).reshape(fields, planes, x_rows, y_cols)


def order_outward(values, across, along):
    fields, planes, x_rows, y_cols = values.shape
    groups = across // along
    rows_each = x_rows // across
    shaped = values.reshape(fields, planes, groups, along, rows_each, y_cols)
    return jnp.swapaxes(shaped, 2, 3).reshape(fields, planes, x_rows, y_cols)


def to_fluid(fields):
    moved = lax.all_to_all(
        lax.all_to_all(fields, "gx", split_axis=3, concat_axis=2, tiled=True),
        "gy",
        split_axis=2,
        concat_axis=2,
        tiled=True,
    )
    return order_inward(moved, lax.axis_size("gx"), lax.axis_size("gy"))


def to_particles(fields):
    ordered = order_outward(fields, lax.axis_size("gx"), lax.axis_size("gy"))
    return lax.all_to_all(
        lax.all_to_all(ordered, "gy", split_axis=2, concat_axis=2, tiled=True),
        "gx",
        split_axis=2,
        concat_axis=3,
        tiled=True,
    )


def shards(particle_count, drag_coeff, particle_velocity, fluid_velocity):
    voids = 1.0 - particle_count.astype(jnp.float32) * particle_volume
    drag_force = drag_coeff[None] * particle_velocity
    slab_velocity = to_particles(fluid_velocity)
    stacked = jnp.concatenate([slab_velocity, voids[None]], axis=0)
    widened = pad_second(padded_2(stacked, ((("gx", "gy"), 2),), 1))
    weights, weight_sum = face_weights(widened[3])
    predicted = momentum(widened[:3], weights, voids, drag_coeff, drag_force)
    flux = voids[None] * predicted
    flux_first = pad_second(padded_2(flux[0:1], ((("gx", "gy"), 2),), 1))
    flux_wide = jnp.concatenate([flux_first, pad_plane(flux[1:3])], axis=0)
    source = divergence(flux_wide)
    pressure = -source / weight_sum
    for sweep_index in range(SWEEPS - 1):
        pressure_wide = pad_second(padded_2(pressure, ((("gx", "gy"), 1),), 1))
        pressure = jacobi_sweep(pressure_wide, weights, weight_sum, source)
    final_wide = pad_second(padded_2(pressure, ((("gx", "gy"), 1),), 1))
    slopes = gradient_of(final_wide)
    velocity = predicted - time_step * slopes
    pressure_out = to_fluid(pressure[None])[0]
    return (pressure_out, velocity, slopes)


def solution(mesh):
    placed = (
        P(None, ("gx", "gy"), None),
        P(None, ("gx", "gy"), None),
        P(None, None, ("gx", "gy"), None),
        P(None, None, "gy", "gx"),
    )
    return jax.shard_map(
        shards,
        mesh=mesh,
        in_specs=placed,
        out_specs=(
            P(None, "gy", "gx"),
            P(None, None, ("gx", "gy"), None),
            P(None, None, ("gx", "gy"), None),
        ),
        check_vma=False,
    )
```

profile of v0, /device:TPU:0, one launch (start us, length us, event | category | flops | bytes accessed | tf_op | source)
XLA Modules:
  0.0 200.9 jit_solution(16246067221753685963)
XLA Ops:
  2.3 26.5 %all_to_all.46 = f32[3,8,64,128]{3,1,0,2:T(8,128)} all-to-all(f32[3,8,64,128]{3,1,0,2:T(8,128)S(1)} %copy.52), channel_id=1, replica_groups=mesh['gx'=8,'gy'=4] {'gy'}, dimensions={2} | all-to-all | bytes 1572864 | tf_op jit(solution)/shard_map/all_to_all | solution.py:137
  28.8 3.7 %all-to-all-start.1 = ((f32[3,8,64,128]{3,1,0,2:T(8,128)}), f32[3,8,64,128]{3,1,0,2:T(8,128)S(1)}, u32[]{:S(2)}, u32[]{:S(2)}) async-start(f32[3,8,64,128]{3,1,0,2:T(8,128)} %all_to_all.46), calls=%async_computation.1 | async-start | bytes 1572864 | tf_op jit(solution)/shard_map/all_to_all | solution.py:136
  32.9 12.2 %all-to-all-done.1 = f32[3,8,64,128]{3,1,0,2:T(8,128)S(1)} async-done(((f32[3,8,64,128]{3,1,0,2:T(8,128)}), f32[3,8,64,128]{3,1,0,2:T(8,128)S(1)}, u32[]{:S(2)}, u32[]{:S(2)}) %all-to-all-start.1) | async-done | bytes 786464 | tf_op jit(solution)/shard_map/all_to_all | solution.py:136
  49.8 4.8 %collective-permute-done.1 = f32[4,8,1,1024]{3,1,2,0:T(8,128)S(1)} collective-permute-done((f32[4,8,1,1024]{3,1,2,0:T(8,128)S(1)}, f32[4,8,1,1024]{3,1,2,0:T(8,128)S(1)}, u32[]{:S(2)}, u32[]{:S(2)}) %collective-permute-start.1) | collective-permute-done | bytes 131104 | tf_op jit(solution)/shard_map/ppermute | solution.py:22
  61.9 4.7 %collective-permute-done.3 = f32[1,8,1,1024]{3,1,2,0:T(8,128)S(1)} collective-permute-done((f32[1,8,1,1024]{3,1,2,0:T(8,128)S(1)}, f32[1,8,1,1024]{3,1,2,0:T(8,128)S(1)}, u32[]{:S(2)}, u32[]{:S(2)}) %collective-permute-start.3) | collective-permute-done | bytes 32800 | tf_op jit(solution)/shard_map/ppermute | solution.py:22
  67.2 3.9 %collective-permute-start.4 = (f32[8,1,1024]{2,0,1:T(8,128)S(1)}, f32[8,1,1024]{2,0,1:T(8,128)S(1)}, u32[]{:S(2)}, u32[]{:S(2)}) collective-permute-start(f32[8,1,1024]{2,0,1:T(8,128)S(1)} %get-tuple-element.46), channel_id=1, source_target_pairs={{0,1},{1,2},{2,3},{3,4},{4,5},{5,6},{6,7},{7,8},{8,9},{9,10},{10,1... | collective-permute-start | bytes 98312 | tf_op jit(solution)/shard_map/ppermute | solution.py:20
  72.7 4.2 %collective-permute-done.5 = f32[8,1,1024]{2,0,1:T(8,128)S(1)} collective-permute-done((f32[8,1,1024]{2,0,1:T(8,128)S(1)}, f32[8,1,1024]{2,0,1:T(8,128)S(1)}, u32[]{:S(2)}, u32[]{:S(2)}) %collective-permute-start.5) | collective-permute-done | bytes 32800 | tf_op jit(solution)/shard_map/ppermute | solution.py:22
  81.4 4.2 %collective-permute-done.7 = f32[8,1,1024]{2,0,1:T(8,128)S(1)} collective-permute-done((f32[8,1,1024]{2,0,1:T(8,128)S(1)}, f32[8,1,1024]{2,0,1:T(8,128)S(1)}, u32[]{:S(2)}, u32[]{:S(2)}) %collective-permute-start.7) | collective-permute-done | bytes 32800 | tf_op jit(solution)/shard_map/ppermute | solution.py:22
  90.8 4.2 %collective-permute-done.9 = f32[8,1,1024]{2,0,1:T(8,128)S(1)} collective-permute-done((f32[8,1,1024]{2,0,1:T(8,128)S(1)}, f32[8,1,1024]{2,0,1:T(8,128)S(1)}, u32[]{:S(2)}, u32[]{:S(2)}) %collective-permute-start.9) | collective-permute-done | bytes 32800 | tf_op jit(solution)/shard_map/ppermute | solution.py:22
  95.6 4.1 %collective-permute-start.10 = (f32[8,1,1024]{2,0,1:T(8,128)S(1)}, f32[8,1,1024]{2,0,1:T(8,128)S(1)}, u32[]{:S(2)}, u32[]{:S(2)}) collective-permute-start(f32[8,1,1024]{2,0,1:T(8,128)S(1)} %get-tuple-element.40), channel_id=1, source_target_pairs={{0,1},{1,2},{2,3},{3,4},{4,5},{5,6},{6,7},{7,8},{8,9},{9,10},{10,1... | collective-permute-start | bytes 98312 | tf_op jit(solution)/shard_map/ppermute | solution.py:20
  101.3 4.6 %collective-permute-done.11 = f32[8,1,1024]{2,0,1:T(8,128)S(1)} collective-permute-done((f32[8,1,1024]{2,0,1:T(8,128)S(1)}, f32[8,1,1024]{2,0,1:T(8,128)S(1)}, u32[]{:S(2)}, u32[]{:S(2)}) %collective-permute-start.11) | collective-permute-done | bytes 32800 | tf_op jit(solution)/shard_map/ppermute | solution.py:22
  106.5 3.9 %collective-permute-start.12 = (f32[8,1,1024]{2,0,1:T(8,128)S(1)}, f32[8,1,1024]{2,0,1:T(8,128)S(1)}, u32[]{:S(2)}, u32[]{:S(2)}) collective-permute-start(f32[8,1,1024]{2,0,1:T(8,128)S(1)} %get-tuple-element.38), channel_id=1, source_target_pairs={{0,1},{1,2},{2,3},{3,4},{4,5},{5,6},{6,7},{7,8},{8,9},{9,10},{10,1... | collective-permute-start | bytes 98312 | tf_op jit(solution)/shard_map/ppermute | solution.py:20
  112.1 4.6 %collective-permute-done.13 = f32[8,1,1024]{2,0,1:T(8,128)S(1)} collective-permute-done((f32[8,1,1024]{2,0,1:T(8,128)S(1)}, f32[8,1,1024]{2,0,1:T(8,128)S(1)}, u32[]{:S(2)}, u32[]{:S(2)}) %collective-permute-start.13) | collective-permute-done | bytes 32800 | tf_op jit(solution)/shard_map/ppermute | solution.py:22
  117.3 3.7 %collective-permute-start.14 = (f32[8,1,1024]{2,0,1:T(8,128)S(1)}, f32[8,1,1024]{2,0,1:T(8,128)S(1)}, u32[]{:S(2)}, u32[]{:S(2)}) collective-permute-start(f32[8,1,1024]{2,0,1:T(8,128)S(1)} %get-tuple-element.36), channel_id=1, source_target_pairs={{0,1},{1,2},{2,3},{3,4},{4,5},{5,6},{6,7},{7,8},{8,9},{9,10},{10,1... | collective-permute-start | bytes 98312 | tf_op jit(solution)/shard_map/ppermute | solution.py:20
  122.6 4.6 %collective-permute-done.15 = f32[8,1,1024]{2,0,1:T(8,128)S(1)} collective-permute-done((f32[8,1,1024]{2,0,1:T(8,128)S(1)}, f32[8,1,1024]{2,0,1:T(8,128)S(1)}, u32[]{:S(2)}, u32[]{:S(2)}) %collective-permute-start.15) | collective-permute-done | bytes 32800 | tf_op jit(solution)/shard_map/ppermute | solution.py:22
  127.7 3.7 %collective-permute-start.16 = (f32[8,1,1024]{2,0,1:T(8,128)S(1)}, f32[8,1,1024]{2,0,1:T(8,128)S(1)}, u32[]{:S(2)}, u32[]{:S(2)}) collective-permute-start(f32[8,1,1024]{2,0,1:T(8,128)S(1)} %get-tuple-element.34), channel_id=1, source_target_pairs={{0,1},{1,2},{2,3},{3,4},{4,5},{5,6},{6,7},{7,8},{8,9},{9,10},{10,1... | collective-permute-start | bytes 98312 | tf_op jit(solution)/shard_map/ppermute | solution.py:20
  133.0 4.6 %collective-permute-done.17 = f32[8,1,1024]{2,0,1:T(8,128)S(1)} collective-permute-done((f32[8,1,1024]{2,0,1:T(8,128)S(1)}, f32[8,1,1024]{2,0,1:T(8,128)S(1)}, u32[]{:S(2)}, u32[]{:S(2)}) %collective-permute-start.17) | collective-permute-done | bytes 32800 | tf_op jit(solution)/shard_map/ppermute | solution.py:22
  139.5 4.5 %collective-permute-start.19 = (f32[8,1,1024]{2,0,1:T(8,128)S(1)}, f32[8,1,1024]{2,0,1:T(8,128)S(1)}, u32[]{:S(2)}, u32[]{:S(2)}) collective-permute-start(f32[8,1,1024]{2,0,1:T(8,128)S(1)} %get-tuple-element.32), channel_id=1, source_target_pairs={{0,1},{1,2},{2,3},{3,4},{4,5},{5,6},{6,7},{7,8},{8,9},{9,10},{10,1... | collective-permute-start | bytes 98312 | tf_op jit(solution)/shard_map/ppermute | solution.py:20
  146.8 4.4 %reshape.29 = f32[8,1,8192]{2,1,0:T(1,128)} reshape(f32[1024,1,8,8]{3,2,1,0:T(8,128)} %bitcast.38) | data formatting | bytes 524288
  151.2 18.5 %all-to-all-start.2 = ((f32[8,1,8192]{2,1,0:T(1,128)}), f32[8,1,8192]{2,1,0:T(1,128)S(1)}, u32[]{:S(2)}, u32[]{:S(2)}) async-start(f32[8,1,8192]{2,1,0:T(1,128)} %reshape.29), calls=%async_computation.2 | async-start | bytes 524288 | tf_op jit(solution)/shard_map/all_to_all | solution.py:125
  169.8 6.7 %all-to-all-done.2 = f32[8,1,8192]{2,1,0:T(1,128)S(1)} async-done(((f32[8,1,8192]{2,1,0:T(1,128)}), f32[8,1,8192]{2,1,0:T(1,128)S(1)}, u32[]{:S(2)}, u32[]{:S(2)}) %all-to-all-start.2) | async-done | bytes 262176 | tf_op jit(solution)/shard_map/all_to_all | solution.py:125
  178.4 4.3 %reshape.30 = f32[1024,1,8,8]{3,2,1,0:T(8,128)} reshape(f32[8,8192]{1,0:T(8,128)S(1)} %reduce) | data formatting | bytes 524288
  186.1 5.7 %all-to-all-start.3 = ((f32[1,8,64,128]{3,1,0,2:T(8,128)}), f32[1,8,64,128]{3,1,0,2:T(8,128)S(1)}, u32[]{:S(2)}, u32[]{:S(2)}) async-start(f32[1,8,64,128]{3,1,0,2:T(8,128)} %bitcast.14), calls=%async_computation.3 | async-start | bytes 524288 | tf_op jit(solution)/shard_map/all_to_all | solution.py:124
  194.9 5.2 %all-to-all-done.3 = f32[1,8,64,128]{3,1,0,2:T(8,128)S(1)} async-done(((f32[1,8,64,128]{3,1,0,2:T(8,128)}), f32[1,8,64,128]{3,1,0,2:T(8,128)S(1)}, u32[]{:S(2)}, u32[]{:S(2)}) %all-to-all-start.3) | async-done | bytes 262176 | tf_op jit(solution)/shard_map/all_to_all | solution.py:124
  (80 shorter events, 48.2 us)
Async XLA Ops:
  2.3 30.2 %copy-start.1 = (f32[8,8,1024]{2,1,0:T(8,128)S(1)}, f32[8,8,1024]{2,1,0:T(8,128)}, u32[]{:S(2)}) copy-start(f32[8,8,1024]{2,1,0:T(8,128)} %param.5) | copy-start | bytes 786436
  28.8 16.3 %all-to-all-start.1 = ((f32[3,8,64,128]{3,1,0,2:T(8,128)}), f32[3,8,64,128]{3,1,0,2:T(8,128)S(1)}, u32[]{:S(2)}, u32[]{:S(2)}) async-start(f32[3,8,64,128]{3,1,0,2:T(8,128)} %all_to_all.46), calls=%async_computation.1 | async-start | bytes 1572864 | tf_op jit(solution)/shard_map/all_to_all | solution.py:136
  45.2 4.6 %collective-permute-start = (f32[4,8,1,1024]{3,1,2,0:T(8,128)S(1)}, f32[4,8,1,1024]{3,1,2,0:T(8,128)S(1)}, u32[]{:S(2)}, u32[]{:S(2)}) collective-permute-start(f32[4,8,1,1024]{3,1,2,0:T(8,128)S(1)} %get-tuple-element.16), channel_id=1, source_target_pairs={{0,1},{1,2},{2,3},{3,4},{4,5},{5,6},{6,7},{7,8},{8,9},{9,10},{10,1... | collective-permute-start | bytes 393224 | tf_op jit(solution)/shard_map/ppermute | solution.py:20
  47.3 7.3 %collective-permute-start.1 = (f32[4,8,1,1024]{3,1,2,0:T(8,128)S(1)}, f32[4,8,1,1024]{3,1,2,0:T(8,128)S(1)}, u32[]{:S(2)}, u32[]{:S(2)}) collective-permute-start(f32[4,8,1,1024]{3,1,2,0:T(8,128)S(1)} %get-tuple-element.17), channel_id=1, source_target_pairs={{1,0},{2,1},{3,2},{4,3},{5,4},{6,5},{7,6},{8,7},{9,8},{10,9},{11,1... | collective-permute-start | bytes 393224 | tf_op jit(solution)/shard_map/ppermute | solution.py:22
  57.8 4.1 %collective-permute-start.2 = (f32[1,8,1,1024]{3,1,2,0:T(8,128)S(1)}, f32[1,8,1,1024]{3,1,2,0:T(8,128)S(1)}, u32[]{:S(2)}, u32[]{:S(2)}) collective-permute-start(f32[1,8,1,1024]{3,1,2,0:T(8,128)S(1)} %get-tuple-element.20), channel_id=1, source_target_pairs={{0,1},{1,2},{2,3},{3,4},{4,5},{5,6},{6,7},{7,8},{8,9},{9,10},{10,1... | collective-permute-start | bytes 98312 | tf_op jit(solution)/shard_map/ppermute | solution.py:20
  60.3 6.3 %collective-permute-start.3 = (f32[1,8,1,1024]{3,1,2,0:T(8,128)S(1)}, f32[1,8,1,1024]{3,1,2,0:T(8,128)S(1)}, u32[]{:S(2)}, u32[]{:S(2)}) collective-permute-start(f32[1,8,1,1024]{3,1,2,0:T(8,128)S(1)} %get-tuple-element.21), channel_id=1, source_target_pairs={{1,0},{2,1},{3,2},{4,3},{5,4},{6,5},{7,6},{8,7},{9,8},{10,9},{11,1... | collective-permute-start | bytes 98312 | tf_op jit(solution)/shard_map/ppermute | solution.py:22
  67.2 5.5 %collective-permute-start.4 = (f32[8,1,1024]{2,0,1:T(8,128)S(1)}, f32[8,1,1024]{2,0,1:T(8,128)S(1)}, u32[]{:S(2)}, u32[]{:S(2)}) collective-permute-start(f32[8,1,1024]{2,0,1:T(8,128)S(1)} %get-tuple-element.46), channel_id=1, source_target_pairs={{0,1},{1,2},{2,3},{3,4},{4,5},{5,6},{6,7},{7,8},{8,9},{9,10},{10,1... | collective-permute-start | bytes 98312 | tf_op jit(solution)/shard_map/ppermute | solution.py:20
  71.2 5.8 %collective-permute-start.5 = (f32[8,1,1024]{2,0,1:T(8,128)S(1)}, f32[8,1,1024]{2,0,1:T(8,128)S(1)}, u32[]{:S(2)}, u32[]{:S(2)}) collective-permute-start(f32[8,1,1024]{2,0,1:T(8,128)S(1)} %get-tuple-element.47), channel_id=1, source_target_pairs={{1,0},{2,1},{3,2},{4,3},{5,4},{6,5},{7,6},{8,7},{9,8},{10,9},{11,1... | collective-permute-start | bytes 98312 | tf_op jit(solution)/shard_map/ppermute | solution.py:22
  77.6 3.8 %collective-permute-start.6 = (f32[8,1,1024]{2,0,1:T(8,128)S(1)}, f32[8,1,1024]{2,0,1:T(8,128)S(1)}, u32[]{:S(2)}, u32[]{:S(2)}) collective-permute-start(f32[8,1,1024]{2,0,1:T(8,128)S(1)} %get-tuple-element.44), channel_id=1, source_target_pairs={{0,1},{1,2},{2,3},{3,4},{4,5},{5,6},{6,7},{7,8},{8,9},{9,10},{10,1... | collective-permute-start | bytes 98312 | tf_op jit(solution)/shard_map/ppermute | solution.py:20
  79.8 5.8 %collective-permute-start.7 = (f32[8,1,1024]{2,0,1:T(8,128)S(1)}, f32[8,1,1024]{2,0,1:T(8,128)S(1)}, u32[]{:S(2)}, u32[]{:S(2)}) collective-permute-start(f32[8,1,1024]{2,0,1:T(8,128)S(1)} %get-tuple-element.45), channel_id=1, source_target_pairs={{1,0},{2,1},{3,2},{4,3},{5,4},{6,5},{7,6},{8,7},{9,8},{10,9},{11,1... | collective-permute-start | bytes 98312 | tf_op jit(solution)/shard_map/ppermute | solution.py:22
  86.3 4.5 %collective-permute-start.8 = (f32[8,1,1024]{2,0,1:T(8,128)S(1)}, f32[8,1,1024]{2,0,1:T(8,128)S(1)}, u32[]{:S(2)}, u32[]{:S(2)}) collective-permute-start(f32[8,1,1024]{2,0,1:T(8,128)S(1)} %get-tuple-element.42), channel_id=1, source_target_pairs={{0,1},{1,2},{2,3},{3,4},{4,5},{5,6},{6,7},{7,8},{8,9},{9,10},{10,1... | collective-permute-start | bytes 98312 | tf_op jit(solution)/shard_map/ppermute | solution.py:20
  89.2 5.8 %collective-permute-start.9 = (f32[8,1,1024]{2,0,1:T(8,128)S(1)}, f32[8,1,1024]{2,0,1:T(8,128)S(1)}, u32[]{:S(2)}, u32[]{:S(2)}) collective-permute-start(f32[8,1,1024]{2,0,1:T(8,128)S(1)} %get-tuple-element.43), channel_id=1, source_target_pairs={{1,0},{2,1},{3,2},{4,3},{5,4},{6,5},{7,6},{8,7},{9,8},{10,9},{11,1... | collective-permute-start | bytes 98312 | tf_op jit(solution)/shard_map/ppermute | solution.py:22
  95.6 5.7 %collective-permute-start.10 = (f32[8,1,1024]{2,0,1:T(8,128)S(1)}, f32[8,1,1024]{2,0,1:T(8,128)S(1)}, u32[]{:S(2)}, u32[]{:S(2)}) collective-permute-start(f32[8,1,1024]{2,0,1:T(8,128)S(1)} %get-tuple-element.40), channel_id=1, source_target_pairs={{0,1},{1,2},{2,3},{3,4},{4,5},{5,6},{6,7},{7,8},{8,9},{9,10},{10,1... | collective-permute-start | bytes 98312 | tf_op jit(solution)/shard_map/ppermute | solution.py:20
  99.7 6.2 %collective-permute-start.11 = (f32[8,1,1024]{2,0,1:T(8,128)S(1)}, f32[8,1,1024]{2,0,1:T(8,128)S(1)}, u32[]{:S(2)}, u32[]{:S(2)}) collective-permute-start(f32[8,1,1024]{2,0,1:T(8,128)S(1)} %get-tuple-element.41), channel_id=1, source_target_pairs={{1,0},{2,1},{3,2},{4,3},{5,4},{6,5},{7,6},{8,7},{9,8},{10,9},{11,1... | collective-permute-start | bytes 98312 | tf_op jit(solution)/shard_map/ppermute | solution.py:22
  106.5 5.5 %collective-permute-start.12 = (f32[8,1,1024]{2,0,1:T(8,128)S(1)}, f32[8,1,1024]{2,0,1:T(8,128)S(1)}, u32[]{:S(2)}, u32[]{:S(2)}) collective-permute-start(f32[8,1,1024]{2,0,1:T(8,128)S(1)} %get-tuple-element.38), channel_id=1, source_target_pairs={{0,1},{1,2},{2,3},{3,4},{4,5},{5,6},{6,7},{7,8},{8,9},{9,10},{10,1... | collective-permute-start | bytes 98312 | tf_op jit(solution)/shard_map/ppermute | solution.py:20
  110.5 6.1 %collective-permute-start.13 = (f32[8,1,1024]{2,0,1:T(8,128)S(1)}, f32[8,1,1024]{2,0,1:T(8,128)S(1)}, u32[]{:S(2)}, u32[]{:S(2)}) collective-permute-start(f32[8,1,1024]{2,0,1:T(8,128)S(1)} %get-tuple-element.39), channel_id=1, source_target_pairs={{1,0},{2,1},{3,2},{4,3},{5,4},{6,5},{7,6},{8,7},{9,8},{10,9},{11,1... | collective-permute-start | bytes 98312 | tf_op jit(solution)/shard_map/ppermute | solution.py:22
  117.3 5.3 %collective-permute-start.14 = (f32[8,1,1024]{2,0,1:T(8,128)S(1)}, f32[8,1,1024]{2,0,1:T(8,128)S(1)}, u32[]{:S(2)}, u32[]{:S(2)}) collective-permute-start(f32[8,1,1024]{2,0,1:T(8,128)S(1)} %get-tuple-element.36), channel_id=1, source_target_pairs={{0,1},{1,2},{2,3},{3,4},{4,5},{5,6},{6,7},{7,8},{8,9},{9,10},{10,1... | collective-permute-start | bytes 98312 | tf_op jit(solution)/shard_map/ppermute | solution.py:20
  121.0 6.1 %collective-permute-start.15 = (f32[8,1,1024]{2,0,1:T(8,128)S(1)}, f32[8,1,1024]{2,0,1:T(8,128)S(1)}, u32[]{:S(2)}, u32[]{:S(2)}) collective-permute-start(f32[8,1,1024]{2,0,1:T(8,128)S(1)} %get-tuple-element.37), channel_id=1, source_target_pairs={{1,0},{2,1},{3,2},{4,3},{5,4},{6,5},{7,6},{8,7},{9,8},{10,9},{11,1... | collective-permute-start | bytes 98312 | tf_op jit(solution)/shard_map/ppermute | solution.py:22
  127.7 5.3 %collective-permute-start.16 = (f32[8,1,1024]{2,0,1:T(8,128)S(1)}, f32[8,1,1024]{2,0,1:T(8,128)S(1)}, u32[]{:S(2)}, u32[]{:S(2)}) collective-permute-start(f32[8,1,1024]{2,0,1:T(8,128)S(1)} %get-tuple-element.34), channel_id=1, source_target_pairs={{0,1},{1,2},{2,3},{3,4},{4,5},{5,6},{6,7},{7,8},{8,9},{9,10},{10,1... | collective-permute-start | bytes 98312 | tf_op jit(solution)/shard_map/ppermute | solution.py:20
  131.5 6.1 %collective-permute-start.17 = (f32[8,1,1024]{2,0,1:T(8,128)S(1)}, f32[8,1,1024]{2,0,1:T(8,128)S(1)}, u32[]{:S(2)}, u32[]{:S(2)}) collective-permute-start(f32[8,1,1024]{2,0,1:T(8,128)S(1)} %get-tuple-element.35), channel_id=1, source_target_pairs={{1,0},{2,1},{3,2},{4,3},{5,4},{6,5},{7,6},{8,7},{9,8},{10,9},{11,1... | collective-permute-start | bytes 98312 | tf_op jit(solution)/shard_map/ppermute | solution.py:22
  138.2 31.4 %collective-permute-start.18 = (f32[8,1,1024]{2,0,1:T(8,128)S(1)}, f32[8,1,1024]{2,0,1:T(8,128)S(1)}, u32[]{:S(2)}, u32[]{:S(2)}) collective-permute-start(f32[8,1,1024]{2,0,1:T(8,128)S(1)} %get-tuple-element.33), channel_id=1, source_target_pairs={{1,0},{2,1},{3,2},{4,3},{5,4},{6,5},{7,6},{8,7},{9,8},{10,9},{11,1... | collective-permute-start | bytes 98312 | tf_op jit(solution)/shard_map/ppermute | solution.py:22
  139.5 30.1 %collective-permute-start.19 = (f32[8,1,1024]{2,0,1:T(8,128)S(1)}, f32[8,1,1024]{2,0,1:T(8,128)S(1)}, u32[]{:S(2)}, u32[]{:S(2)}) collective-permute-start(f32[8,1,1024]{2,0,1:T(8,128)S(1)} %get-tuple-element.32), channel_id=1, source_target_pairs={{0,1},{1,2},{2,3},{3,4},{4,5},{5,6},{6,7},{7,8},{8,9},{9,10},{10,1... | collective-permute-start | bytes 98312 | tf_op jit(solution)/shard_map/ppermute | solution.py:20
  151.2 25.4 %all-to-all-start.2 = ((f32[8,1,8192]{2,1,0:T(1,128)}), f32[8,1,8192]{2,1,0:T(1,128)S(1)}, u32[]{:S(2)}, u32[]{:S(2)}) async-start(f32[8,1,8192]{2,1,0:T(1,128)} %reshape.29), calls=%async_computation.2 | async-start | bytes 524288 | tf_op jit(solution)/shard_map/all_to_all | solution.py:125
  186.1 14.0 %all-to-all-start.3 = ((f32[1,8,64,128]{3,1,0,2:T(8,128)}), f32[1,8,64,128]{3,1,0,2:T(8,128)S(1)}, u32[]{:S(2)}, u32[]{:S(2)}) async-start(f32[1,8,64,128]{3,1,0,2:T(8,128)} %bitcast.14), calls=%async_computation.3 | async-start | bytes 524288 | tf_op jit(solution)/shard_map/all_to_all | solution.py:124
  (2 other events, 31.4 us)
where the time goes:
time: 202 us; the launch traced here: 201 us
  starting transfers between devices  74.5 us (37%)
  waiting for transfers between devices  67.8 us (34%)
  blocking collectives  26.5 us (13%)
  local copies, waits for them, and re-layouts  21.6 us (11%)
  other arithmetic  9.39 us (5%)
    ppermute x10, waiting for transfers between devices, padded_2(): lax.ppermute(head, axis, [((i + 1) % count, i) for i in range(ends)])  40.5 us
    ppermute x10, starting transfers between devices, padded_2(): lax.ppermute(tail, axis, [(i, (i + 1) % count) for i in range(ends)])  33.7 us
    all_to_all x1, blocking collectives, to_particles(): lax.all_to_all(ordered, 'gy', split_axis=2, concat_axis=2, tiled=True)  26.5 us
    all_to_all x1, starting transfers between devices, to_fluid(): lax.all_to_all(fields, 'gx', split_axis=3, concat_axis=2, tiled=True)  18.5 us
    ppermute x10, starting transfers between devices, padded_2(): lax.ppermute(head, axis, [((i + 1) % count, i) for i in range(ends)])  12.9 us
    all_to_all x1, waiting for transfers between devices, to_particles(): lax.all_to_all(lax.all_to_all(ordered, 'gy', split_axis=2, concat_axis=2,...  12.2 us
    unnamed x10, local copies, waits for them, and re-layouts  12.1 us
    all_to_all x1, waiting for transfers between devices, to_fluid(): lax.all_to_all(fields, 'gx', split_axis=3, concat_axis=2, tiled=True)  6.72 us
  transfers between devices with their start and end apart: 23, of which 20 were waited for; matrix products, arithmetic and copies ran while one was open for 5% of the time, Pallas kernels for 0%

commit v1 on v0

--- a/solution.py
+++ b/solution.py
@@ -7,6 +7,29 @@
 particle_volume = 0.05
 time_step = 0.5
 viscosity = 0.1
+
+
+def in_blocks(array, dim, size):
+    shape = array.shape
+    parts = array.reshape(*shape[:dim], size, shape[dim] // size, *shape[dim + 1 :])
+    return jnp.moveaxis(parts, dim, 0)
+
+
+def joined_along(blocks, dim):
+    blocks = jnp.moveaxis(blocks, 0, dim)
+    shape = blocks.shape
+    return blocks.reshape(*shape[:dim], shape[dim] * shape[dim + 1], *shape[dim + 2 :])
+
+
+def exchange_directly(array, axis, split_dim, concat_dim):
+    size, here = (lax.axis_size(axis), lax.axis_index(axis))
+    blocks = in_blocks(array, split_dim, size)
+    finished = [blocks[here]]
+    for lap in range(1, size):
+        sent = blocks[(here + lap) % size]
+        finished.append(lax.ppermute(sent, axis, [(i, (i + lap) % size) for i in range(size)]))
+    blocks = jnp.stack(finished)[(here - jnp.arange(size)) % size]
+    return joined_along(blocks, concat_dim)
 
 
 def padded_2(cells, sides, width):
@@ -122,11 +145,7 @@
 
 def to_fluid(fields):
     moved = lax.all_to_all(
-        lax.all_to_all(fields, "gx", split_axis=3, concat_axis=2, tiled=True),
-        "gy",
-        split_axis=2,
-        concat_axis=2,
-        tiled=True,
+        exchange_directly(fields, "gx", 3, 2), "gy", split_axis=2, concat_axis=2, tiled=True
     )
     return order_inward(moved, lax.axis_size("gx"), lax.axis_size("gy"))
 

time: 202 us -> 191 us (0.946)
  local copies, waits for them, and re-layouts: 21.6 us -> 5.81 us
  starting transfers between devices: 74.5 us -> 79.6 us
  waiting for transfers between devices: 67.8 us -> 64.3 us
  other arithmetic: 9.39 us -> 12.1 us
    ppermute x0 -> x7, starting transfers between devices: none -> 25.7 us  [exchange_directly(): lax.ppermute(sent, axis, [(i, (i + lap) % size) for i in range(size)])]
    all_to_all x2 -> x1, starting transfers between devices: 24.2 us -> 3.41 us  [to_fluid(): lax.all_to_all(exchange_directly(fields, 'gx', 3, 2), 'gy', split_axis=2,...]
    unnamed x10 -> x13, local copies, waits for them, and re-layouts: 12.1 us -> 0.71 us
    all_to_all x2 -> x1, waiting for transfers between devices: 11.9 us -> 7.13 us  [to_fluid(): lax.all_to_all(exchange_directly(fields, 'gx', 3, 2), 'gy', split_axis=2,...]
    all_to_all x3 -> x1, local copies, waits for them, and re-layouts: 4.02 us -> 0.05 us  [to_fluid(): lax.all_to_all(exchange_directly(fields, 'gx', 3, 2), 'gy', split_axis=2,...]
    concatenate x9, other arithmetic: 1.73 us -> 4.76 us  [padded_2(): jnp.concatenate([lax.ppermute(tail, axis, [(i, (i + 1) % count) for i in...]
    broadcast_in_dim x1 -> x0, local copies, waits for them, and re-layouts: 2.66 us -> none  [shards(): pressure_out = to_fluid(pressure[None])[0]]
  transfers between devices with their start and end apart: 23 -> 29, of which waited for: 20 -> 20; matrix products, arithmetic and copies ran while one was open for 5% -> 1% of each run, Pallas kernels for 0% -> 0%
where the time goes in v1:
time: 191 us; the launch traced here: 189 us
  starting transfers between devices  79.6 us (42%)
  waiting for transfers between devices  64.3 us (34%)
  blocking collectives  26.4 us (14%)
  other arithmetic  12.1 us (6%)
  local copies, waits for them, and re-layouts  5.81 us (3%)
    ppermute x10, waiting for transfers between devices, padded_2(): lax.ppermute(head, axis, [((i + 1) % count, i) for i in range(ends)])  40.3 us
    ppermute x10, starting transfers between devices, padded_2(): lax.ppermute(tail, axis, [(i, (i + 1) % count) for i in range(ends)])  33.7 us
    all_to_all x1, blocking collectives, to_particles(): lax.all_to_all(ordered, 'gy', split_axis=2, concat_axis=2, tiled=True)  26.4 us
    ppermute x7, starting transfers between devices, exchange_directly(): lax.ppermute(sent, axis, [(i, (i + lap) % size) for i in range(size)])  25.7 us
    ppermute x10, starting transfers between devices, padded_2(): lax.ppermute(head, axis, [((i + 1) % count, i) for i in range(ends)])  13.1 us
    all_to_all x1, waiting for transfers between devices, to_particles(): lax.all_to_all(lax.all_to_all(ordered, 'gy', split_axis=2, concat_axis=2,...  12.5 us
    all_to_all x1, waiting for transfers between devices, to_fluid(): lax.all_to_all(exchange_directly(fields, 'gx', 3, 2), 'gy', split_axis=2,...  7.13 us
    concatenate x9, other arithmetic, padded_2(): jnp.concatenate([lax.ppermute(tail, axis, [(i, (i + 1) % count) for i in...  4.76 us
  transfers between devices with their start and end apart: 29, of which 20 were waited for; matrix products, arithmetic and copies ran while one was open for 1% of the time, Pallas kernels for 0%

profile of v1, /device:TPU:0, one launch (start us, length us, event | category | flops | bytes accessed | tf_op | source)
XLA Modules:
  0.0 189.4 jit_solution(1856491226234648268)
XLA Ops:
  2.3 26.4 %all_to_all.28 = f32[3,8,64,128]{3,1,0,2:T(8,128)} all-to-all(f32[3,8,64,128]{3,1,0,2:T(8,128)S(1)} %copy.19), channel_id=1, replica_groups=mesh['gx'=8,'gy'=4] {'gy'}, dimensions={2} | all-to-all | bytes 1572864 | tf_op jit(solution)/shard_map/all_to_all | solution.py:156
  28.7 3.7 %all-to-all-start.1 = ((f32[3,8,64,128]{3,1,0,2:T(8,128)}), f32[3,8,64,128]{3,1,0,2:T(8,128)S(1)}, u32[]{:S(2)}, u32[]{:S(2)}) async-start(f32[3,8,64,128]{3,1,0,2:T(8,128)} %all_to_all.28), calls=%async_computation.1 | async-start | bytes 1572864 | tf_op jit(solution)/shard_map/all_to_all | solution.py:155
  32.5 12.5 %all-to-all-done.1 = f32[3,8,64,128]{3,1,0,2:T(8,128)S(1)} async-done(((f32[3,8,64,128]{3,1,0,2:T(8,128)}), f32[3,8,64,128]{3,1,0,2:T(8,128)S(1)}, u32[]{:S(2)}, u32[]{:S(2)}) %all-to-all-start.1) | async-done | bytes 786464 | tf_op jit(solution)/shard_map/all_to_all | solution.py:155
  49.9 4.8 %collective-permute-done.1 = f32[4,8,1,1024]{3,2,1,0:T(1,128)S(1)} collective-permute-done((f32[4,8,1,1024]{3,2,1,0:T(1,128)S(1)}, f32[4,8,1,1024]{3,2,1,0:T(1,128)S(1)}, u32[]{:S(2)}, u32[]{:S(2)}) %collective-permute-start.1) | collective-permute-done | bytes 131104 | tf_op jit(solution)/shard_map/ppermute | solution.py:45
  63.1 4.5 %collective-permute-done.3 = f32[1,8,1,1024]{3,2,1,0:T(1,128)S(1)} collective-permute-done((f32[1,8,1,1024]{3,2,1,0:T(1,128)S(1)}, f32[1,8,1,1024]{3,2,1,0:T(1,128)S(1)}, u32[]{:S(2)}, u32[]{:S(2)}) %collective-permute-start.3) | collective-permute-done | bytes 32800 | tf_op jit(solution)/shard_map/ppermute | solution.py:45
  68.5 3.9 %collective-permute-start.4 = (f32[8,1,1024]{2,1,0:T(1,128)S(1)}, f32[8,1,1024]{2,1,0:T(1,128)S(1)}, u32[]{:S(2)}, u32[]{:S(2)}) collective-permute-start(f32[8,1,1024]{2,1,0:T(1,128)S(1)} %get-tuple-element.44), channel_id=1, source_target_pairs={{0,1},{1,2},{2,3},{3,4},{4,5},{5,6},{6,7},{7,8},{8,9},{9,10},{10,1... | collective-permute-start | bytes 98312 | tf_op jit(solution)/shard_map/ppermute | solution.py:43
  74.0 4.2 %collective-permute-done.5 = f32[8,1,1024]{2,1,0:T(1,128)S(1)} collective-permute-done((f32[8,1,1024]{2,1,0:T(1,128)S(1)}, f32[8,1,1024]{2,1,0:T(1,128)S(1)}, u32[]{:S(2)}, u32[]{:S(2)}) %collective-permute-start.5) | collective-permute-done | bytes 32800 | tf_op jit(solution)/shard_map/ppermute | solution.py:45
  83.0 4.2 %collective-permute-done.7 = f32[8,1,1024]{2,1,0:T(1,128)S(1)} collective-permute-done((f32[8,1,1024]{2,1,0:T(1,128)S(1)}, f32[8,1,1024]{2,1,0:T(1,128)S(1)}, u32[]{:S(2)}, u32[]{:S(2)}) %collective-permute-start.7) | collective-permute-done | bytes 32800 | tf_op jit(solution)/shard_map/ppermute | solution.py:45
  92.6 4.2 %collective-permute-done.9 = f32[8,1,1024]{2,1,0:T(1,128)S(1)} collective-permute-done((f32[8,1,1024]{2,1,0:T(1,128)S(1)}, f32[8,1,1024]{2,1,0:T(1,128)S(1)}, u32[]{:S(2)}, u32[]{:S(2)}) %collective-permute-start.9) | collective-permute-done | bytes 32800 | tf_op jit(solution)/shard_map/ppermute | solution.py:45
  97.7 4.1 %collective-permute-start.10 = (f32[8,1,1024]{2,1,0:T(1,128)S(1)}, f32[8,1,1024]{2,1,0:T(1,128)S(1)}, u32[]{:S(2)}, u32[]{:S(2)}) collective-permute-start(f32[8,1,1024]{2,1,0:T(1,128)S(1)} %get-tuple-element.38), channel_id=1, source_target_pairs={{0,1},{1,2},{2,3},{3,4},{4,5},{5,6},{6,7},{7,8},{8,9},{9,10},{10,1... | collective-permute-start | bytes 98312 | tf_op jit(solution)/shard_map/ppermute | solution.py:43
  103.4 4.6 %collective-permute-done.11 = f32[8,1,1024]{2,1,0:T(1,128)S(1)} collective-permute-done((f32[8,1,1024]{2,1,0:T(1,128)S(1)}, f32[8,1,1024]{2,1,0:T(1,128)S(1)}, u32[]{:S(2)}, u32[]{:S(2)}) %collective-permute-start.11) | collective-permute-done | bytes 32800 | tf_op jit(solution)/shard_map/ppermute | solution.py:45
  108.9 3.9 %collective-permute-start.12 = (f32[8,1,1024]{2,1,0:T(1,128)S(1)}, f32[8,1,1024]{2,1,0:T(1,128)S(1)}, u32[]{:S(2)}, u32[]{:S(2)}) collective-permute-start(f32[8,1,1024]{2,1,0:T(1,128)S(1)} %get-tuple-element.36), channel_id=1, source_target_pairs={{0,1},{1,2},{2,3},{3,4},{4,5},{5,6},{6,7},{7,8},{8,9},{9,10},{10,1... | collective-permute-start | bytes 98312 | tf_op jit(solution)/shard_map/ppermute | solution.py:43
  114.4 4.6 %collective-permute-done.13 = f32[8,1,1024]{2,1,0:T(1,128)S(1)} collective-permute-done((f32[8,1,1024]{2,1,0:T(1,128)S(1)}, f32[8,1,1024]{2,1,0:T(1,128)S(1)}, u32[]{:S(2)}, u32[]{:S(2)}) %collective-permute-start.13) | collective-permute-done | bytes 32800 | tf_op jit(solution)/shard_map/ppermute | solution.py:45
  119.8 3.7 %collective-permute-start.14 = (f32[8,1,1024]{2,1,0:T(1,128)S(1)}, f32[8,1,1024]{2,1,0:T(1,128)S(1)}, u32[]{:S(2)}, u32[]{:S(2)}) collective-permute-start(f32[8,1,1024]{2,1,0:T(1,128)S(1)} %get-tuple-element.34), channel_id=1, source_target_pairs={{0,1},{1,2},{2,3},{3,4},{4,5},{5,6},{6,7},{7,8},{8,9},{9,10},{10,1... | collective-permute-start | bytes 98312 | tf_op jit(solution)/shard_map/ppermute | solution.py:43
  125.1 4.6 %collective-permute-done.15 = f32[8,1,1024]{2,1,0:T(1,128)S(1)} collective-permute-done((f32[8,1,1024]{2,1,0:T(1,128)S(1)}, f32[8,1,1024]{2,1,0:T(1,128)S(1)}, u32[]{:S(2)}, u32[]{:S(2)}) %collective-permute-start.15) | collective-permute-done | bytes 32800 | tf_op jit(solution)/shard_map/ppermute | solution.py:45
  130.6 3.7 %collective-permute-start.16 = (f32[8,1,1024]{2,1,0:T(1,128)S(1)}, f32[8,1,1024]{2,1,0:T(1,128)S(1)}, u32[]{:S(2)}, u32[]{:S(2)}) collective-permute-start(f32[8,1,1024]{2,1,0:T(1,128)S(1)} %get-tuple-element.32), channel_id=1, source_target_pairs={{0,1},{1,2},{2,3},{3,4},{4,5},{5,6},{6,7},{7,8},{8,9},{9,10},{10,1... | collective-permute-start | bytes 98312 | tf_op jit(solution)/shard_map/ppermute | solution.py:43
  135.9 4.6 %collective-permute-done.17 = f32[8,1,1024]{2,1,0:T(1,128)S(1)} collective-permute-done((f32[8,1,1024]{2,1,0:T(1,128)S(1)}, f32[8,1,1024]{2,1,0:T(1,128)S(1)}, u32[]{:S(2)}, u32[]{:S(2)}) %collective-permute-start.17) | collective-permute-done | bytes 32800 | tf_op jit(solution)/shard_map/ppermute | solution.py:45
  142.6 4.5 %collective-permute-start.26 = (f32[8,1,1024]{2,1,0:T(1,128)S(1)}, f32[8,1,1024]{2,1,0:T(1,128)S(1)}, u32[]{:S(2)}, u32[]{:S(2)}) collective-permute-start(f32[8,1,1024]{2,1,0:T(1,128)S(1)} %get-tuple-element.23), channel_id=1, source_target_pairs={{0,1},{1,2},{2,3},{3,4},{4,5},{5,6},{6,7},{7,8},{8,9},{9,10},{10,1... | collective-permute-start | bytes 98312 | tf_op jit(solution)/shard_map/ppermute | solution.py:43
  147.2 4.0 %collective-permute-start.18 = (f32[1,8,8,128]{3,2,1,0:T(8,128)S(1)}, f32[1,8,8,128]{3,2,1,0:T(8,128)S(1)}, u32[]{:S(2)}, u32[]{:S(2)}) collective-permute-start(f32[1,8,8,128]{3,2,1,0:T(8,128)S(1)} %get-tuple-element.31), channel_id=1, source_target_pairs={{0,4},{4,8},{8,12},{12,16},{16,20},{20,24},{24,28},{28,0},{1,5},{5... | collective-permute-start | bytes 98312 | tf_op jit(solution)/shard_map/ppermute | solution.py:30
  151.2 7.7 %collective-permute-start.19 = (f32[1,8,8,128]{3,2,1,0:T(8,128)S(1)}, f32[1,8,8,128]{3,2,1,0:T(8,128)S(1)}, u32[]{:S(2)}, u32[]{:S(2)}) collective-permute-start(f32[1,8,8,128]{3,2,1,0:T(8,128)S(1)} %get-tuple-element.30), channel_id=1, source_target_pairs={{0,8},{4,12},{8,16},{12,20},{16,24},{20,28},{24,0},{28,4},{1,9},{5... | collective-permute-start | bytes 98312 | tf_op jit(solution)/shard_map/ppermute | solution.py:30
  158.8 7.1 %collective-permute-start.20 = (f32[1,8,8,128]{3,2,1,0:T(8,128)S(1)}, f32[1,8,8,128]{3,2,1,0:T(8,128)S(1)}, u32[]{:S(2)}, u32[]{:S(2)}) collective-permute-start(f32[1,8,8,128]{3,2,1,0:T(8,128)S(1)} %get-tuple-element.29), channel_id=1, source_target_pairs={{0,12},{4,16},{8,20},{12,24},{16,28},{20,0},{24,4},{28,8},{1,13},{... | collective-permute-start | bytes 98312 | tf_op jit(solution)/shard_map/ppermute | solution.py:30
  169.9 3.7 %collective-permute-start.24 = (f32[1,8,8,128]{3,2,1,0:T(8,128)S(1)}, f32[1,8,8,128]{3,2,1,0:T(8,128)S(1)}, u32[]{:S(2)}, u32[]{:S(2)}) collective-permute-start(f32[1,8,8,128]{3,2,1,0:T(8,128)S(1)} %get-tuple-element.25), channel_id=1, source_target_pairs={{0,28},{4,0},{8,4},{12,8},{16,12},{20,16},{24,20},{28,24},{1,29},{... | collective-permute-start | bytes 98312 | tf_op jit(solution)/shard_map/ppermute | solution.py:30
  176.6 3.4 %all-to-all-start.2 = ((f32[1,8,64,128]{3,1,0,2:T(8,128)}), f32[1,8,64,128]{3,1,0,2:T(8,128)S(1)}, u32[]{:S(2)}, u32[]{:S(2)}) async-start(f32[1,8,64,128]{3,1,0,2:T(8,128)} %copy.30), calls=%async_computation.2 | async-start | bytes 524288 | tf_op jit(solution)/shard_map/all_to_all | solution.py:147
  181.5 7.1 %all-to-all-done.2 = f32[1,8,64,128]{3,1,0,2:T(8,128)S(1)} async-done(((f32[1,8,64,128]{3,1,0,2:T(8,128)}), f32[1,8,64,128]{3,1,0,2:T(8,128)S(1)}, u32[]{:S(2)}, u32[]{:S(2)}) %all-to-all-start.2) | async-done | bytes 262176 | tf_op jit(solution)/shard_map/all_to_all | solution.py:147
  (99 shorter events, 48.4 us)
Async XLA Ops:
  28.7 16.3 %all-to-all-start.1 = ((f32[3,8,64,128]{3,1,0,2:T(8,128)}), f32[3,8,64,128]{3,1,0,2:T(8,128)S(1)}, u32[]{:S(2)}, u32[]{:S(2)}) async-start(f32[3,8,64,128]{3,1,0,2:T(8,128)} %all_to_all.28), calls=%async_computation.1 | async-start | bytes 1572864 | tf_op jit(solution)/shard_map/all_to_all | solution.py:155
  47.4 7.3 %collective-permute-start.1 = (f32[4,8,1,1024]{3,2,1,0:T(1,128)S(1)}, f32[4,8,1,1024]{3,2,1,0:T(1,128)S(1)}, u32[]{:S(2)}, u32[]{:S(2)}) collective-permute-start(f32[4,8,1,1024]{3,2,1,0:T(1,128)S(1)} %get-tuple-element.10), channel_id=1, source_target_pairs={{1,0},{2,1},{3,2},{4,3},{5,4},{6,5},{7,6},{8,7},{9,8},{10,9},{11,1... | collective-permute-start | bytes 393224 | tf_op jit(solution)/shard_map/ppermute | solution.py:45
  61.4 6.3 %collective-permute-start.3 = (f32[1,8,1,1024]{3,2,1,0:T(1,128)S(1)}, f32[1,8,1,1024]{3,2,1,0:T(1,128)S(1)}, u32[]{:S(2)}, u32[]{:S(2)}) collective-permute-start(f32[1,8,1,1024]{3,2,1,0:T(1,128)S(1)} %get-tuple-element.12), channel_id=1, source_target_pairs={{1,0},{2,1},{3,2},{4,3},{5,4},{6,5},{7,6},{8,7},{9,8},{10,9},{11,1... | collective-permute-start | bytes 98312 | tf_op jit(solution)/shard_map/ppermute | solution.py:45
  68.5 5.5 %collective-permute-start.4 = (f32[8,1,1024]{2,1,0:T(1,128)S(1)}, f32[8,1,1024]{2,1,0:T(1,128)S(1)}, u32[]{:S(2)}, u32[]{:S(2)}) collective-permute-start(f32[8,1,1024]{2,1,0:T(1,128)S(1)} %get-tuple-element.44), channel_id=1, source_target_pairs={{0,1},{1,2},{2,3},{3,4},{4,5},{5,6},{6,7},{7,8},{8,9},{9,10},{10,1... | collective-permute-start | bytes 98312 | tf_op jit(solution)/shard_map/ppermute | solution.py:43
  72.5 5.8 %collective-permute-start.5 = (f32[8,1,1024]{2,1,0:T(1,128)S(1)}, f32[8,1,1024]{2,1,0:T(1,128)S(1)}, u32[]{:S(2)}, u32[]{:S(2)}) collective-permute-start(f32[8,1,1024]{2,1,0:T(1,128)S(1)} %get-tuple-element.45), channel_id=1, source_target_pairs={{1,0},{2,1},{3,2},{4,3},{5,4},{6,5},{7,6},{8,7},{9,8},{10,9},{11,1... | collective-permute-start | bytes 98312 | tf_op jit(solution)/shard_map/ppermute | solution.py:45
  81.4 5.8 %collective-permute-start.7 = (f32[8,1,1024]{2,1,0:T(1,128)S(1)}, f32[8,1,1024]{2,1,0:T(1,128)S(1)}, u32[]{:S(2)}, u32[]{:S(2)}) collective-permute-start(f32[8,1,1024]{2,1,0:T(1,128)S(1)} %get-tuple-element.43), channel_id=1, source_target_pairs={{1,0},{2,1},{3,2},{4,3},{5,4},{6,5},{7,6},{8,7},{9,8},{10,9},{11,1... | collective-permute-start | bytes 98312 | tf_op jit(solution)/shard_map/ppermute | solution.py:45
  91.0 5.8 %collective-permute-start.9 = (f32[8,1,1024]{2,1,0:T(1,128)S(1)}, f32[8,1,1024]{2,1,0:T(1,128)S(1)}, u32[]{:S(2)}, u32[]{:S(2)}) collective-permute-start(f32[8,1,1024]{2,1,0:T(1,128)S(1)} %get-tuple-element.41), channel_id=1, source_target_pairs={{1,0},{2,1},{3,2},{4,3},{5,4},{6,5},{7,6},{8,7},{9,8},{10,9},{11,1... | collective-permute-start | bytes 98312 | tf_op jit(solution)/shard_map/ppermute | solution.py:45
  97.7 5.7 %collective-permute-start.10 = (f32[8,1,1024]{2,1,0:T(1,128)S(1)}, f32[8,1,1024]{2,1,0:T(1,128)S(1)}, u32[]{:S(2)}, u32[]{:S(2)}) collective-permute-start(f32[8,1,1024]{2,1,0:T(1,128)S(1)} %get-tuple-element.38), channel_id=1, source_target_pairs={{0,1},{1,2},{2,3},{3,4},{4,5},{5,6},{6,7},{7,8},{8,9},{9,10},{10,1... | collective-permute-start | bytes 98312 | tf_op jit(solution)/shard_map/ppermute | solution.py:43
  101.8 6.2 %collective-permute-start.11 = (f32[8,1,1024]{2,1,0:T(1,128)S(1)}, f32[8,1,1024]{2,1,0:T(1,128)S(1)}, u32[]{:S(2)}, u32[]{:S(2)}) collective-permute-start(f32[8,1,1024]{2,1,0:T(1,128)S(1)} %get-tuple-element.39), channel_id=1, source_target_pairs={{1,0},{2,1},{3,2},{4,3},{5,4},{6,5},{7,6},{8,7},{9,8},{10,9},{11,1... | collective-permute-start | bytes 98312 | tf_op jit(solution)/shard_map/ppermute | solution.py:45
  108.9 5.5 %collective-permute-start.12 = (f32[8,1,1024]{2,1,0:T(1,128)S(1)}, f32[8,1,1024]{2,1,0:T(1,128)S(1)}, u32[]{:S(2)}, u32[]{:S(2)}) collective-permute-start(f32[8,1,1024]{2,1,0:T(1,128)S(1)} %get-tuple-element.36), channel_id=1, source_target_pairs={{0,1},{1,2},{2,3},{3,4},{4,5},{5,6},{6,7},{7,8},{8,9},{9,10},{10,1... | collective-permute-start | bytes 98312 | tf_op jit(solution)/shard_map/ppermute | solution.py:43
  112.8 6.1 %collective-permute-start.13 = (f32[8,1,1024]{2,1,0:T(1,128)S(1)}, f32[8,1,1024]{2,1,0:T(1,128)S(1)}, u32[]{:S(2)}, u32[]{:S(2)}) collective-permute-start(f32[8,1,1024]{2,1,0:T(1,128)S(1)} %get-tuple-element.37), channel_id=1, source_target_pairs={{1,0},{2,1},{3,2},{4,3},{5,4},{6,5},{7,6},{8,7},{9,8},{10,9},{11,1... | collective-permute-start | bytes 98312 | tf_op jit(solution)/shard_map/ppermute | solution.py:45
  119.8 5.3 %collective-permute-start.14 = (f32[8,1,1024]{2,1,0:T(1,128)S(1)}, f32[8,1,1024]{2,1,0:T(1,128)S(1)}, u32[]{:S(2)}, u32[]{:S(2)}) collective-permute-start(f32[8,1,1024]{2,1,0:T(1,128)S(1)} %get-tuple-element.34), channel_id=1, source_target_pairs={{0,1},{1,2},{2,3},{3,4},{4,5},{5,6},{6,7},{7,8},{8,9},{9,10},{10,1... | collective-permute-start | bytes 98312 | tf_op jit(solution)/shard_map/ppermute | solution.py:43
  123.5 6.1 %collective-permute-start.15 = (f32[8,1,1024]{2,1,0:T(1,128)S(1)}, f32[8,1,1024]{2,1,0:T(1,128)S(1)}, u32[]{:S(2)}, u32[]{:S(2)}) collective-permute-start(f32[8,1,1024]{2,1,0:T(1,128)S(1)} %get-tuple-element.35), channel_id=1, source_target_pairs={{1,0},{2,1},{3,2},{4,3},{5,4},{6,5},{7,6},{8,7},{9,8},{10,9},{11,1... | collective-permute-start | bytes 98312 | tf_op jit(solution)/shard_map/ppermute | solution.py:45
  130.6 5.3 %collective-permute-start.16 = (f32[8,1,1024]{2,1,0:T(1,128)S(1)}, f32[8,1,1024]{2,1,0:T(1,128)S(1)}, u32[]{:S(2)}, u32[]{:S(2)}) collective-permute-start(f32[8,1,1024]{2,1,0:T(1,128)S(1)} %get-tuple-element.32), channel_id=1, source_target_pairs={{0,1},{1,2},{2,3},{3,4},{4,5},{5,6},{6,7},{7,8},{8,9},{9,10},{10,1... | collective-permute-start | bytes 98312 | tf_op jit(solution)/shard_map/ppermute | solution.py:43
  134.3 6.1 %collective-permute-start.17 = (f32[8,1,1024]{2,1,0:T(1,128)S(1)}, f32[8,1,1024]{2,1,0:T(1,128)S(1)}, u32[]{:S(2)}, u32[]{:S(2)}) collective-permute-start(f32[8,1,1024]{2,1,0:T(1,128)S(1)} %get-tuple-element.33), channel_id=1, source_target_pairs={{1,0},{2,1},{3,2},{4,3},{5,4},{6,5},{7,6},{8,7},{9,8},{10,9},{11,1... | collective-permute-start | bytes 98312 | tf_op jit(solution)/shard_map/ppermute | solution.py:45
  141.3 24.6 %collective-permute-start.25 = (f32[8,1,1024]{2,1,0:T(1,128)S(1)}, f32[8,1,1024]{2,1,0:T(1,128)S(1)}, u32[]{:S(2)}, u32[]{:S(2)}) collective-permute-start(f32[8,1,1024]{2,1,0:T(1,128)S(1)} %get-tuple-element.24), channel_id=1, source_target_pairs={{1,0},{2,1},{3,2},{4,3},{5,4},{6,5},{7,6},{8,7},{9,8},{10,9},{11,1... | collective-permute-start | bytes 98312 | tf_op jit(solution)/shard_map/ppermute | solution.py:45
  142.6 23.3 %collective-permute-start.26 = (f32[8,1,1024]{2,1,0:T(1,128)S(1)}, f32[8,1,1024]{2,1,0:T(1,128)S(1)}, u32[]{:S(2)}, u32[]{:S(2)}) collective-permute-start(f32[8,1,1024]{2,1,0:T(1,128)S(1)} %get-tuple-element.23), channel_id=1, source_target_pairs={{0,1},{1,2},{2,3},{3,4},{4,5},{5,6},{6,7},{7,8},{8,9},{9,10},{10,1... | collective-permute-start | bytes 98312 | tf_op jit(solution)/shard_map/ppermute | solution.py:43
  147.2 20.8 %collective-permute-start.18 = (f32[1,8,8,128]{3,2,1,0:T(8,128)S(1)}, f32[1,8,8,128]{3,2,1,0:T(8,128)S(1)}, u32[]{:S(2)}, u32[]{:S(2)}) collective-permute-start(f32[1,8,8,128]{3,2,1,0:T(8,128)S(1)} %get-tuple-element.31), channel_id=1, source_target_pairs={{0,4},{4,8},{8,12},{12,16},{16,20},{20,24},{24,28},{28,0},{1,5},{5... | collective-permute-start | bytes 98312 | tf_op jit(solution)/shard_map/ppermute | solution.py:30
  151.2 18.7 %collective-permute-start.19 = (f32[1,8,8,128]{3,2,1,0:T(8,128)S(1)}, f32[1,8,8,128]{3,2,1,0:T(8,128)S(1)}, u32[]{:S(2)}, u32[]{:S(2)}) collective-permute-start(f32[1,8,8,128]{3,2,1,0:T(8,128)S(1)} %get-tuple-element.30), channel_id=1, source_target_pairs={{0,8},{4,12},{8,16},{12,20},{16,24},{20,28},{24,0},{28,4},{1,9},{5... | collective-permute-start | bytes 98312 | tf_op jit(solution)/shard_map/ppermute | solution.py:30
  158.8 14.8 %collective-permute-start.20 = (f32[1,8,8,128]{3,2,1,0:T(8,128)S(1)}, f32[1,8,8,128]{3,2,1,0:T(8,128)S(1)}, u32[]{:S(2)}, u32[]{:S(2)}) collective-permute-start(f32[1,8,8,128]{3,2,1,0:T(8,128)S(1)} %get-tuple-element.29), channel_id=1, source_target_pairs={{0,12},{4,16},{8,20},{12,24},{16,28},{20,0},{24,4},{28,8},{1,13},{... | collective-permute-start | bytes 98312 | tf_op jit(solution)/shard_map/ppermute | solution.py:30
  165.9 7.7 %collective-permute-start.21 = (f32[1,8,8,128]{3,2,1,0:T(8,128)S(1)}, f32[1,8,8,128]{3,2,1,0:T(8,128)S(1)}, u32[]{:S(2)}, u32[]{:S(2)}) collective-permute-start(f32[1,8,8,128]{3,2,1,0:T(8,128)S(1)} %get-tuple-element.28), channel_id=1, source_target_pairs={{0,16},{4,20},{8,24},{12,28},{16,0},{20,4},{24,8},{28,12},{1,17},{... | collective-permute-start | bytes 98312 | tf_op jit(solution)/shard_map/ppermute | solution.py:30
  165.9 7.7 %collective-permute-start.22 = (f32[1,8,8,128]{3,2,1,0:T(8,128)S(1)}, f32[1,8,8,128]{3,2,1,0:T(8,128)S(1)}, u32[]{:S(2)}, u32[]{:S(2)}) collective-permute-start(f32[1,8,8,128]{3,2,1,0:T(8,128)S(1)} %get-tuple-element.27), channel_id=1, source_target_pairs={{0,20},{4,24},{8,28},{12,0},{16,4},{20,8},{24,12},{28,16},{1,21},{... | collective-permute-start | bytes 98312 | tf_op jit(solution)/shard_map/ppermute | solution.py:30
  168.0 5.6 %collective-permute-start.23 = (f32[1,8,8,128]{3,2,1,0:T(8,128)S(1)}, f32[1,8,8,128]{3,2,1,0:T(8,128)S(1)}, u32[]{:S(2)}, u32[]{:S(2)}) collective-permute-start(f32[1,8,8,128]{3,2,1,0:T(8,128)S(1)} %get-tuple-element.26), channel_id=1, source_target_pairs={{0,24},{4,28},{8,0},{12,4},{16,8},{20,12},{24,16},{28,20},{1,25},{... | collective-permute-start | bytes 98312 | tf_op jit(solution)/shard_map/ppermute | solution.py:30
  176.6 11.9 %all-to-all-start.2 = ((f32[1,8,64,128]{3,1,0,2:T(8,128)}), f32[1,8,64,128]{3,1,0,2:T(8,128)S(1)}, u32[]{:S(2)}, u32[]{:S(2)}) async-start(f32[1,8,64,128]{3,1,0,2:T(8,128)} %copy.30), calls=%async_computation.2 | async-start | bytes 524288 | tf_op jit(solution)/shard_map/all_to_all | solution.py:147
  (8 other events, 84.7 us)
